TPU v7x, 128 devices: a whole 4x4x4 slice. The times are simulated.
128 devices in a mesh: dom: 16 (over x, y_lo, core), cls: 8 (over y_hi, z).
Axes of the slice: x: 4, y: 4 (y_hi: 2, y_lo: 2; y = y_hi * 2 + y_lo), z: 4, core: 2. Of those that a mesh axis runs over, the one named last changes fastest.
Arguments:
- particles: bfloat16 [256, 16640], P('dom'), may hold values from -5 to 5
- references: bfloat16 [16, 16, 16640], P('dom', 'cls'), may hold values from -0.15504342 to 0.15504342
- inv_noise: float32 [8320], replicated, may hold values from 0.3 to 3
- shifts: int32 [128, 2], replicated, may hold values from -5 to 5, as said below
- prior_class: int32 [256], P('dom'), may hold values from 0 to 15
- prior_orient: int32 [256], P('dom'), may hold values from 0 to 15
Outputs:
- back_projection: float32 [16, 16, 16640], P('dom', 'cls')
- class_weights: float32 [16, 16], P('dom', 'cls')
- log_norm: float32 [256], P('dom')
Inputs may be any that keep to these rules, and one draw needn't show every extreme that they name: `shifts`: row 0 is the zero translation and row 1 is (5, -5).
All inputs are finite; a program needn't handle non-finite values.
Results may differ from a plain program's by a relative error of at most 0.0022.
Values may be sent and summed in bfloat16 or wider, within the bound.
A program may use at most 64 MiB of HBM per device.

v0:
```python
import math
import jax
import jax.numpy as jnp
from jax import lax
from jax.sharding import PartitionSpec as P

L = 128
PRIOR_LOG_BOOST = 12.0


def from_root(block, axis, owner):
    block = jnp.where(lax.axis_index(axis) == owner, block, jnp.zeros_like(block))
    return lax.psum(block, axis)


def combined_all(part, axis, combine):
    gathered = jax.tree.map(lambda a: lax.all_gather(a, axis), part)

    def take(source):
        return jax.tree.map(lambda a: lax.dynamic_index_in_dim(a, source, 0, False), gathered)

    return lax.fori_loop(
        1, lax.axis_size(axis), lambda source, state: combine(state, take(source)), take(0)
    )


def phase_table(shifts):
    half_width = L // 2 + 1
    row_index = jnp.arange(L, dtype=jnp.int32)
    freq_y = jnp.where(row_index < L // 2, row_index, row_index - L)
    freq_y = jnp.repeat(freq_y, half_width)
    freq_x = jnp.tile(jnp.arange(half_width, dtype=jnp.int32), L)
    phase_turns = (freq_x[:, None] * shifts[None, :, 0] + freq_y[:, None] * shifts[None, :, 1]) % L
    shift_phase_radians = phase_turns.astype(jnp.float32) * (2.0 * math.pi / L)
    return jnp.concatenate([jnp.cos(shift_phase_radians), jnp.sin(shift_phase_radians)], 0).astype(
        jnp.bfloat16
    )


def correlate(reference_block, parts_real, parts_imag, inv_noise, table):
    width = parts_real.shape[1]
    ref_real = reference_block[:, :width].astype(jnp.float32)
    ref_imag = reference_block[:, width:].astype(jnp.float32)
    prod_real = inv_noise * (
        parts_real[:, None, :] * ref_real[None] + parts_imag[:, None, :] * ref_imag[None]
    )
    prod_imag = inv_noise * (
        parts_imag[:, None, :] * ref_real[None] - parts_real[:, None, :] * ref_imag[None]
    )
    products = jnp.concatenate([prod_real, prod_imag], -1).astype(jnp.bfloat16)
    row_count = parts_real.shape[0]
    orient_count = reference_block.shape[0]
    score_grid = jnp.dot(
        products.reshape(row_count * orient_count, 2 * width),
        table,
        preferred_element_type=jnp.float32,
    )
    score_grid = score_grid.reshape(row_count, orient_count, table.shape[1])
    power = 0.5 * jnp.sum(inv_noise * (ref_real * ref_real + ref_imag * ref_imag), -1)
    return score_grid - power[None, :, None]


def project_back(posterior_floor, parts_real, parts_imag, table):
    width = parts_real.shape[1]
    row_count, orient_count, trans_count = posterior_floor.shape
    coeff = jnp.dot(
        posterior_floor.reshape(row_count * orient_count, trans_count),
        table.T,
        preferred_element_type=jnp.float32,
    )
    coeff = coeff.reshape(row_count, orient_count, 2 * width)
    cos_sum = coeff[:, :, :width]
    sin_sum = coeff[:, :, width:]
    real_part = jnp.sum(parts_real[:, None, :] * cos_sum + parts_imag[:, None, :] * sin_sum, 0)
    imag_part = jnp.sum(parts_imag[:, None, :] * cos_sum - parts_real[:, None, :] * sin_sum, 0)
    return jnp.concatenate([real_part, imag_part], -1)


def lse_combine(first, second):
    top = jnp.maximum(first[0], second[0])
    return (top, first[1] * jnp.exp(first[0] - top) + second[1] * jnp.exp(second[0] - top))


def on_device(particles, references, inv_noise, shifts, prior_class, prior_orient):
    table = phase_table(shifts)
    width = inv_noise.shape[0]
    parts_real = particles[:, :width].astype(jnp.float32)
    parts_imag = particles[:, width:].astype(jnp.float32)
    slots = references.shape[0]
    orient_count = references.shape[1]
    part_count = particles.shape[0]
    trans_count = table.shape[1]
    domain_groups = lax.axis_size("dom")
    classes = slots * domain_groups
    orient_ids = lax.axis_index("cls") * orient_count + jnp.arange(orient_count, dtype=jnp.int32)
    orient_hit = prior_orient[:, None] == orient_ids[None, :]

    def score_class(class_id, carry):
        stored, run_top, run_total = carry
        mine = lax.dynamic_index_in_dim(references, class_id % slots, 0, keepdims=False)
        refs_class = from_root(mine, "dom", class_id // slots)
        score_grid = correlate(refs_class, parts_real, parts_imag, inv_noise, table)
        best_match = orient_hit & (prior_class[:, None] == class_id)
        score_grid = (
            score_grid + jnp.where(best_match, PRIOR_LOG_BOOST, 0.0).astype(jnp.float32)[:, :, None]
        )
        stored = lax.dynamic_update_index_in_dim(stored, score_grid, class_id, 0)
        local_top = jnp.max(score_grid, axis=(1, 2))
        local_total = jnp.sum(jnp.exp(score_grid - local_top[:, None, None]), axis=(1, 2))
        class_top, class_total = combined_all((local_top, local_total), "cls", lse_combine)
        run_top, run_total = lse_combine((run_top, run_total), (class_top, class_total))
        return (stored, run_top, run_total)

    start_carry = (
        jnp.zeros((classes, part_count, orient_count, trans_count), jnp.float32),
        jnp.full((part_count,), -1e30, jnp.float32),
        jnp.zeros((part_count,), jnp.float32),
    )
    stored, run_top, run_total = lax.fori_loop(0, classes, score_class, start_carry)
    top, total = (run_top, run_total)
    log_norm = top + jnp.log(total)

    def back_class(class_id):
        posterior = jnp.exp(stored[class_id] - log_norm[:, None, None])
        weight = jnp.sum(posterior, axis=(0, 2))
        sums = project_back(posterior.astype(jnp.bfloat16), parts_real, parts_imag, table)
        return (sums, weight)

    sums_all, weight_all = lax.map(back_class, jnp.arange(classes, dtype=jnp.int32))
    back_projection, class_weights = (
        lax.psum_scatter(sums_all, "dom", scatter_dimension=0, tiled=True),
        lax.psum_scatter(weight_all, "dom", scatter_dimension=0, tiled=True),
    )
    return (back_projection, class_weights, log_norm)


def solution(mesh):
    placed = (P("dom", None), P("dom", "cls", None), P(), P(), P("dom"), P("dom"))
    return jax.shard_map(
        on_device,
        mesh=mesh,
        in_specs=placed,
        out_specs=(P("dom", "cls", None), P("dom", "cls"), P("dom")),
        check_vma=False,
    )
```

profile of v0, /device:TPU:1, one launch (start us, length us, event | category | flops | bytes accessed | tf_op | source)
XLA Modules:
  0.0 2455.8 jit_solution(5740838051703521263)
XLA Ops:
  45.7 2152.6 %while.91 = (s32[]{:T(128)}, f32[16,16,2,128]{3,1,2,0:T(8,128)S(1)}, f32[16]{0:T(128)S(1)}, f32[16]{0:T(128)S(1)}, f32[8320]{0:T(1024)S(1)}, /*index=5*/f32[16,8...) while((s32[]{:T(128)}, ...), condition=%wide.region_7.8_spmd.clone, body=%wide.region_0.7_spmd.clone.sunk | while | flops 141344560 | bytes 8527440 | solution.py:119
  47.9 110.5 %all-reduce.14.cloned.1.call-done = bf16[2,16640]{1,0:T(2,128)(2,1)} async-done(((bf16[2,16640]{1,0:T(2,128)(2,1)}), bf16[2,16640]{1,0:T(2,128)(2,1)}) %all-reduce.14.cloned.1.call-update) | async-done | bytes 66576 | tf_op jit(solution)/shard_map/while/body/eval_jaxpr/psum | solution.py:13
  164.4 20.5 all-reduce.8
  187.5 105.3 %all-reduce.14.cloned.1.call-done = bf16[2,16640]{1,0:T(2,128)(2,1)} async-done(((bf16[2,16640]{1,0:T(2,128)(2,1)}), bf16[2,16640]{1,0:T(2,128)(2,1)}) %all-reduce.14.cloned.1.call-update) | async-done | bytes 66576 | tf_op jit(solution)/shard_map/while/body/eval_jaxpr/psum | solution.py:13
  298.8 20.5 all-reduce.8
  321.9 105.3 %all-reduce.14.cloned.1.call-done = bf16[2,16640]{1,0:T(2,128)(2,1)} async-done(((bf16[2,16640]{1,0:T(2,128)(2,1)}), bf16[2,16640]{1,0:T(2,128)(2,1)}) %all-reduce.14.cloned.1.call-update) | async-done | bytes 66576 | tf_op jit(solution)/shard_map/while/body/eval_jaxpr/psum | solution.py:13
  456.3 105.0 %all-reduce.14.cloned.1.call-done = bf16[2,16640]{1,0:T(2,128)(2,1)} async-done(((bf16[2,16640]{1,0:T(2,128)(2,1)}), bf16[2,16640]{1,0:T(2,128)(2,1)}) %all-reduce.14.cloned.1.call-update) | async-done | bytes 66576 | tf_op jit(solution)/shard_map/while/body/eval_jaxpr/psum | solution.py:13
  590.4 104.9 %all-reduce.14.cloned.1.call-done = bf16[2,16640]{1,0:T(2,128)(2,1)} async-done(((bf16[2,16640]{1,0:T(2,128)(2,1)}), bf16[2,16640]{1,0:T(2,128)(2,1)}) %all-reduce.14.cloned.1.call-update) | async-done | bytes 66576 | tf_op jit(solution)/shard_map/while/body/eval_jaxpr/psum | solution.py:13
  724.4 104.9 %all-reduce.14.cloned.1.call-done = bf16[2,16640]{1,0:T(2,128)(2,1)} async-done(((bf16[2,16640]{1,0:T(2,128)(2,1)}), bf16[2,16640]{1,0:T(2,128)(2,1)}) %all-reduce.14.cloned.1.call-update) | async-done | bytes 66576 | tf_op jit(solution)/shard_map/while/body/eval_jaxpr/psum | solution.py:13
  858.4 105.3 %all-reduce.14.cloned.1.call-done = bf16[2,16640]{1,0:T(2,128)(2,1)} async-done(((bf16[2,16640]{1,0:T(2,128)(2,1)}), bf16[2,16640]{1,0:T(2,128)(2,1)}) %all-reduce.14.cloned.1.call-update) | async-done | bytes 66576 | tf_op jit(solution)/shard_map/while/body/eval_jaxpr/psum | solution.py:13
  992.8 105.3 %all-reduce.14.cloned.1.call-done = bf16[2,16640]{1,0:T(2,128)(2,1)} async-done(((bf16[2,16640]{1,0:T(2,128)(2,1)}), bf16[2,16640]{1,0:T(2,128)(2,1)}) %all-reduce.14.cloned.1.call-update) | async-done | bytes 66576 | tf_op jit(solution)/shard_map/while/body/eval_jaxpr/psum | solution.py:13
  1104.0 20.5 all-reduce.8
  1127.2 105.3 %all-reduce.14.cloned.1.call-done = bf16[2,16640]{1,0:T(2,128)(2,1)} async-done(((bf16[2,16640]{1,0:T(2,128)(2,1)}), bf16[2,16640]{1,0:T(2,128)(2,1)}) %all-reduce.14.cloned.1.call-update) | async-done | bytes 66576 | tf_op jit(solution)/shard_map/while/body/eval_jaxpr/psum | solution.py:13
  1261.5 105.0 %all-reduce.14.cloned.1.call-done = bf16[2,16640]{1,0:T(2,128)(2,1)} async-done(((bf16[2,16640]{1,0:T(2,128)(2,1)}), bf16[2,16640]{1,0:T(2,128)(2,1)}) %all-reduce.14.cloned.1.call-update) | async-done | bytes 66576 | tf_op jit(solution)/shard_map/while/body/eval_jaxpr/psum | solution.py:13
  1395.6 105.3 %all-reduce.14.cloned.1.call-done = bf16[2,16640]{1,0:T(2,128)(2,1)} async-done(((bf16[2,16640]{1,0:T(2,128)(2,1)}), bf16[2,16640]{1,0:T(2,128)(2,1)}) %all-reduce.14.cloned.1.call-update) | async-done | bytes 66576 | tf_op jit(solution)/shard_map/while/body/eval_jaxpr/psum | solution.py:13
  1530.0 105.0 %all-reduce.14.cloned.1.call-done = bf16[2,16640]{1,0:T(2,128)(2,1)} async-done(((bf16[2,16640]{1,0:T(2,128)(2,1)}), bf16[2,16640]{1,0:T(2,128)(2,1)}) %all-reduce.14.cloned.1.call-update) | async-done | bytes 66576 | tf_op jit(solution)/shard_map/while/body/eval_jaxpr/psum | solution.py:13
  1664.0 105.3 %all-reduce.14.cloned.1.call-done = bf16[2,16640]{1,0:T(2,128)(2,1)} async-done(((bf16[2,16640]{1,0:T(2,128)(2,1)}), bf16[2,16640]{1,0:T(2,128)(2,1)}) %all-reduce.14.cloned.1.call-update) | async-done | bytes 66576 | tf_op jit(solution)/shard_map/while/body/eval_jaxpr/psum | solution.py:13
  1798.4 104.9 %all-reduce.14.cloned.1.call-done = bf16[2,16640]{1,0:T(2,128)(2,1)} async-done(((bf16[2,16640]{1,0:T(2,128)(2,1)}), bf16[2,16640]{1,0:T(2,128)(2,1)}) %all-reduce.14.cloned.1.call-update) | async-done | bytes 66576 | tf_op jit(solution)/shard_map/while/body/eval_jaxpr/psum | solution.py:13
  1932.4 105.0 %all-reduce.14.cloned.1.call-done = bf16[2,16640]{1,0:T(2,128)(2,1)} async-done(((bf16[2,16640]{1,0:T(2,128)(2,1)}), bf16[2,16640]{1,0:T(2,128)(2,1)}) %all-reduce.14.cloned.1.call-update) | async-done | bytes 66576 | tf_op jit(solution)/shard_map/while/body/eval_jaxpr/psum | solution.py:13
  2066.5 105.0 %all-reduce.14.cloned.1.call-done = bf16[2,16640]{1,0:T(2,128)(2,1)} async-done(((bf16[2,16640]{1,0:T(2,128)(2,1)}), bf16[2,16640]{1,0:T(2,128)(2,1)}) %all-reduce.14.cloned.1.call-update) | async-done | bytes 66576 | tf_op jit(solution)/shard_map/while/body/eval_jaxpr/psum | solution.py:13
  2177.4 20.5 all-reduce.8
  2198.5 126.5 %while.89 = (s32[]{:T(128)}, f32[16,2,16640]{2,1,0:T(2,128)}, f32[16,2]{1,0:T(8,128)S(1)}, f32[16,8320]{1,0:T(8,128)S(1)}, s32[16]{0:T(128)S(1)}, /*index=5*/f32...) while((s32[]{:T(128)}, f32[16,2,16640]{2,1,0:T(2,128)}, ...), condition=%wide.region_12.13_spmd, body=%wide.region_8.12_spmd.sunk | while | flops 138461184 | bytes 10018055 | solution.py:129
  2326.2 31.8 %all-reduce.5 = f32[16,2]{1,0:T(8,128)S(1)} all-reduce(f32[16,2]{1,0:T(8,128)S(1)} %get-tuple-element.556), channel_id=5, replica_groups=mesh['dom'=16,'cls'=8] {'dom'}, use_global_device_ids=true, to_apply=%region_14.15.clone | all-reduce | flops 32 | bytes 256
  2359.1 87.3 %all-reduce.12.cloned.1.call-done = f32[16,2,16640]{2,1,0:T(2,128)} async-done(((f32[16,2,16640]{2,1,0:T(2,128)}), f32[16,2,16640]{2,1,0:T(2,128)}) %all-reduce.12.cloned.1.call-update) | async-done | bytes 2129936
  (592 shorter events, 512.3 us)
Async XLA Ops:
  28.6 17.1 copy-start
  28.6 17.1 copy-start.1
  28.6 17.1 copy-start.3
  28.6 17.1 copy-start.4
  28.6 17.1 copy-start.6
  45.7 112.7 %all-reduce.14.cloned.1.call-start = ((), (), s32[]{:S(2)}) async-start(), calls=%async_computation.1 | async-start | bytes 133120 | tf_op jit(solution)/shard_map/while/body/eval_jaxpr/psum | solution.py:13
  185.4 107.4 %all-reduce.14.cloned.1.call-start = ((), (), s32[]{:S(2)}) async-start(), calls=%async_computation.1 | async-start | bytes 133120 | tf_op jit(solution)/shard_map/while/body/eval_jaxpr/psum | solution.py:13
  319.8 107.4 %all-reduce.14.cloned.1.call-start = ((), (), s32[]{:S(2)}) async-start(), calls=%async_computation.1 | async-start | bytes 133120 | tf_op jit(solution)/shard_map/while/body/eval_jaxpr/psum | solution.py:13
  454.1 107.1 %all-reduce.14.cloned.1.call-start = ((), (), s32[]{:S(2)}) async-start(), calls=%async_computation.1 | async-start | bytes 133120 | tf_op jit(solution)/shard_map/while/body/eval_jaxpr/psum | solution.py:13
  588.2 107.1 %all-reduce.14.cloned.1.call-start = ((), (), s32[]{:S(2)}) async-start(), calls=%async_computation.1 | async-start | bytes 133120 | tf_op jit(solution)/shard_map/while/body/eval_jaxpr/psum | solution.py:13
  722.2 107.1 %all-reduce.14.cloned.1.call-start = ((), (), s32[]{:S(2)}) async-start(), calls=%async_computation.1 | async-start | bytes 133120 | tf_op jit(solution)/shard_map/while/body/eval_jaxpr/psum | solution.py:13
  856.3 107.4 %all-reduce.14.cloned.1.call-start = ((), (), s32[]{:S(2)}) async-start(), calls=%async_computation.1 | async-start | bytes 133120 | tf_op jit(solution)/shard_map/while/body/eval_jaxpr/psum | solution.py:13
  990.7 107.4 %all-reduce.14.cloned.1.call-start = ((), (), s32[]{:S(2)}) async-start(), calls=%async_computation.1 | async-start | bytes 133120 | tf_op jit(solution)/shard_map/while/body/eval_jaxpr/psum | solution.py:13
  1125.0 107.4 %all-reduce.14.cloned.1.call-start = ((), (), s32[]{:S(2)}) async-start(), calls=%async_computation.1 | async-start | bytes 133120 | tf_op jit(solution)/shard_map/while/body/eval_jaxpr/psum | solution.py:13
  1259.4 107.1 %all-reduce.14.cloned.1.call-start = ((), (), s32[]{:S(2)}) async-start(), calls=%async_computation.1 | async-start | bytes 133120 | tf_op jit(solution)/shard_map/while/body/eval_jaxpr/psum | solution.py:13
  1393.5 107.4 %all-reduce.14.cloned.1.call-start = ((), (), s32[]{:S(2)}) async-start(), calls=%async_computation.1 | async-start | bytes 133120 | tf_op jit(solution)/shard_map/while/body/eval_jaxpr/psum | solution.py:13
  1527.8 107.1 %all-reduce.14.cloned.1.call-start = ((), (), s32[]{:S(2)}) async-start(), calls=%async_computation.1 | async-start | bytes 133120 | tf_op jit(solution)/shard_map/while/body/eval_jaxpr/psum | solution.py:13
  1661.9 107.4 %all-reduce.14.cloned.1.call-start = ((), (), s32[]{:S(2)}) async-start(), calls=%async_computation.1 | async-start | bytes 133120 | tf_op jit(solution)/shard_map/while/body/eval_jaxpr/psum | solution.py:13
  1796.2 107.1 %all-reduce.14.cloned.1.call-start = ((), (), s32[]{:S(2)}) async-start(), calls=%async_computation.1 | async-start | bytes 133120 | tf_op jit(solution)/shard_map/while/body/eval_jaxpr/psum | solution.py:13
  1930.3 107.1 %all-reduce.14.cloned.1.call-start = ((), (), s32[]{:S(2)}) async-start(), calls=%async_computation.1 | async-start | bytes 133120 | tf_op jit(solution)/shard_map/while/body/eval_jaxpr/psum | solution.py:13
  2064.3 107.1 %all-reduce.14.cloned.1.call-start = ((), (), s32[]{:S(2)}) async-start(), calls=%async_computation.1 | async-start | bytes 133120 | tf_op jit(solution)/shard_map/while/body/eval_jaxpr/psum | solution.py:13
  2198.4 248.1 %all-reduce.12.cloned.1.call-start = ((), (), s32[]{:S(2)}) async-start(), calls=%async_computation | async-start | bytes 4259840
  2324.9 123.7 %copy-start.2 = (f32[16]{0:T(128)}, f32[16]{0:T(128)S(1)}, u32[]{:S(2)}) copy-start(f32[16]{0:T(128)S(1)} %get-tuple-element.1018) | copy-start | bytes 196
  2325.0 0.7 copy-start.5
Sparse Core Ops, SparseCore 0:
  49.8 108.6 all-reduce.13
  189.4 103.3 all-reduce.13
  323.8 103.3 all-reduce.13
  457.9 103.3 all-reduce.13
  591.9 103.3 all-reduce.13
  726.0 103.3 all-reduce.13
  860.3 103.3 all-reduce.13
  994.7 103.3 all-reduce.13
  1129.1 103.3 all-reduce.13
  1263.1 103.3 all-reduce.13
  1397.5 103.3 all-reduce.13
  1531.5 103.3 all-reduce.13
  1665.9 103.3 all-reduce.13
  1799.9 103.3 all-reduce.13
  1934.0 103.3 all-reduce.13
  2068.0 103.3 all-reduce.13
Sparse Core Ops, SparseCore 1:
  2325.1 121.3 all-reduce.11
where the time goes:
time: 2460 us
  waiting for transfers between devices  1770 us (72%)
  blocking collectives  360 us (15%)
  other arithmetic  115 us (5%)
  matrix products  110 us (4%)
  loops' own time  44.6 us (2%)
  local copies, waits for them, and re-layouts  35.7 us (1%)
    psum x16, waiting for transfers between devices, from_root(): return lax.psum(block, axis)  1690 us
    while x16, blocking collectives  328 us
    unnamed x2, waiting for transfers between devices  87.3 us
    dot_general x16, matrix products, project_back(): jnp.dot(posterior_floor.reshape(row_count * orient_count, trans_count), t...  61.1 us
  transfers between devices with their start and end apart: 17, of which 17 were waited for; matrix products, arithmetic and copies ran while one was open for 1% of the time, Pallas kernels for 0%

commit v1 on v0

--- a/solution.py
+++ b/solution.py
@@ -10,7 +10,7 @@
 
 def from_root(block, axis, owner):
     block = jnp.where(lax.axis_index(axis) == owner, block, jnp.zeros_like(block))
-    return lax.psum(block, axis)
+    return jnp.sum(lax.all_gather(block, axis), axis=0)
 
 
 def combined_all(part, axis, combine):

time: 2460 us -> 1310 us (0.53)
  waiting for transfers between devices: 1770 us -> 622 us
    psum x16 -> x0, waiting for transfers between devices: 1690 us -> none  [from_root(): return lax.psum(block, axis)]
    all_gather x0 -> x16, waiting for transfers between devices: none -> 532 us  [from_root(): return jnp.sum(lax.all_gather(block, axis), axis=0)]
    reduce_sum x0 -> x16, other arithmetic: none -> 34.6 us  [from_root(): return jnp.sum(lax.all_gather(block, axis), axis=0)]
where the time goes in v1:
time: 1310 us
  waiting for transfers between devices  622 us (47%)
  blocking collectives  356 us (27%)
  other arithmetic  125 us (10%)
  matrix products  110 us (8%)
  loops' own time  45.6 us (3%)
  local copies, waits for them, and re-layouts  35.8 us (3%)
  between operations  15.3 us (1%)
    all_gather x16, waiting for transfers between devices, from_root(): return jnp.sum(lax.all_gather(block, axis), axis=0)  532 us
    while x16, blocking collectives  325 us
    unnamed x2, waiting for transfers between devices  89.2 us
    dot_general x16, matrix products, project_back(): jnp.dot(posterior_floor.reshape(row_count * orient_count, trans_count), t...  61.1 us
    dot_general x16, matrix products, correlate(): jnp.dot(products.reshape(row_count * orient_count, 2 * width), table, pre...  48.5 us
    reduce_sum x16, other arithmetic, from_root(): return jnp.sum(lax.all_gather(block, axis), axis=0)  34.6 us
    another operation x1, loops' own time, on_device(): lax.map(back_class, jnp.arange(classes, dtype=jnp.int32))  31.3 us
    unnamed x1, blocking collectives  31.1 us
  transfers between devices with their start and end apart: 17, of which 17 were waited for; matrix products, arithmetic and copies ran while one was open for 1% of the time, Pallas kernels for 0%

profile of v1, /device:TPU:1, one launch (start us, length us, event | category | flops | bytes accessed | tf_op | source)
XLA Modules:
  0.0 1309.8 jit_solution(6439659741350930152)
XLA Ops:
  45.7 1005.4 %while.91 = (s32[]{:T(128)}, f32[16,16,2,128]{3,1,2,0:T(8,128)S(1)}, f32[16]{0:T(128)S(1)}, f32[16]{0:T(128)S(1)}, f32[8320]{0:T(1024)S(1)}, /*index=5*/f32[16,8...) while((s32[]{:T(128)}, ...), condition=%wide.region_7.8_spmd.clone, body=%wide.region_0.7_spmd.clone.sunk | while | flops 141810480 | bytes 12654170 | solution.py:119
  48.0 37.2 %all-gather.4.cloned.1.call-done = bf16[16,2,16640]{2,1,0:T(2,128)(2,1)} async-done(((bf16[1,2,16640]{2,1,0:T(2,128)(2,1)}), bf16[16,2,16640]{2,1,0:T(2,128)(2,1)}) %all-gather.4.cloned.1.call-update) | async-done | bytes 1064976 | tf_op jit(solution)/shard_map/while/body/eval_jaxpr/all_gather | solution.py:13
  114.7 33.2 %all-gather.4.cloned.1.call-done = bf16[16,2,16640]{2,1,0:T(2,128)(2,1)} async-done(((bf16[1,2,16640]{2,1,0:T(2,128)(2,1)}), bf16[16,2,16640]{2,1,0:T(2,128)(2,1)}) %all-gather.4.cloned.1.call-update) | async-done | bytes 1064976 | tf_op jit(solution)/shard_map/while/body/eval_jaxpr/all_gather | solution.py:13
  177.4 33.2 %all-gather.4.cloned.1.call-done = bf16[16,2,16640]{2,1,0:T(2,128)(2,1)} async-done(((bf16[1,2,16640]{2,1,0:T(2,128)(2,1)}), bf16[16,2,16640]{2,1,0:T(2,128)(2,1)}) %all-gather.4.cloned.1.call-update) | async-done | bytes 1064976 | tf_op jit(solution)/shard_map/while/body/eval_jaxpr/all_gather | solution.py:13
  240.2 32.9 %all-gather.4.cloned.1.call-done = bf16[16,2,16640]{2,1,0:T(2,128)(2,1)} async-done(((bf16[1,2,16640]{2,1,0:T(2,128)(2,1)}), bf16[16,2,16640]{2,1,0:T(2,128)(2,1)}) %all-gather.4.cloned.1.call-update) | async-done | bytes 1064976 | tf_op jit(solution)/shard_map/while/body/eval_jaxpr/all_gather | solution.py:13
  302.6 32.9 %all-gather.4.cloned.1.call-done = bf16[16,2,16640]{2,1,0:T(2,128)(2,1)} async-done(((bf16[1,2,16640]{2,1,0:T(2,128)(2,1)}), bf16[16,2,16640]{2,1,0:T(2,128)(2,1)}) %all-gather.4.cloned.1.call-update) | async-done | bytes 1064976 | tf_op jit(solution)/shard_map/while/body/eval_jaxpr/all_gather | solution.py:13
  365.1 32.9 %all-gather.4.cloned.1.call-done = bf16[16,2,16640]{2,1,0:T(2,128)(2,1)} async-done(((bf16[1,2,16640]{2,1,0:T(2,128)(2,1)}), bf16[16,2,16640]{2,1,0:T(2,128)(2,1)}) %all-gather.4.cloned.1.call-update) | async-done | bytes 1064976 | tf_op jit(solution)/shard_map/while/body/eval_jaxpr/all_gather | solution.py:13
  404.5 20.3 %all-reduce.8 = (f32[128]{0:T(128)S(1)}, f32[128]{0:T(128)S(1)}) all-reduce(f32[128]{0:T(128)S(1)} %dynamic-update-slice.6, f32[128]{0:T(128)S(1)} %dynamic-update-slice.7), channel_id=2, replica_groups=mesh['dom'=16,'cls'=8] {'cls'}, use_global_device_ids=true, to_apply=%add | all-reduce | flops 256 | bytes 2048 | tf_op jit(solution)/shard_map/while
  427.5 33.2 %all-gather.4.cloned.1.call-done = bf16[16,2,16640]{2,1,0:T(2,128)(2,1)} async-done(((bf16[1,2,16640]{2,1,0:T(2,128)(2,1)}), bf16[16,2,16640]{2,1,0:T(2,128)(2,1)}) %all-gather.4.cloned.1.call-update) | async-done | bytes 1064976 | tf_op jit(solution)/shard_map/while/body/eval_jaxpr/all_gather | solution.py:13
  490.2 33.2 %all-gather.4.cloned.1.call-done = bf16[16,2,16640]{2,1,0:T(2,128)(2,1)} async-done(((bf16[1,2,16640]{2,1,0:T(2,128)(2,1)}), bf16[16,2,16640]{2,1,0:T(2,128)(2,1)}) %all-gather.4.cloned.1.call-update) | async-done | bytes 1064976 | tf_op jit(solution)/shard_map/while/body/eval_jaxpr/all_gather | solution.py:13
  553.0 33.2 %all-gather.4.cloned.1.call-done = bf16[16,2,16640]{2,1,0:T(2,128)(2,1)} async-done(((bf16[1,2,16640]{2,1,0:T(2,128)(2,1)}), bf16[16,2,16640]{2,1,0:T(2,128)(2,1)}) %all-gather.4.cloned.1.call-update) | async-done | bytes 1064976 | tf_op jit(solution)/shard_map/while/body/eval_jaxpr/all_gather | solution.py:13
  592.7 20.3 %all-reduce.8 = (f32[128]{0:T(128)S(1)}, f32[128]{0:T(128)S(1)}) all-reduce(f32[128]{0:T(128)S(1)} %dynamic-update-slice.6, f32[128]{0:T(128)S(1)} %dynamic-update-slice.7), channel_id=2, replica_groups=mesh['dom'=16,'cls'=8] {'cls'}, use_global_device_ids=true, to_apply=%add | all-reduce | flops 256 | bytes 2048 | tf_op jit(solution)/shard_map/while
  615.7 32.9 %all-gather.4.cloned.1.call-done = bf16[16,2,16640]{2,1,0:T(2,128)(2,1)} async-done(((bf16[1,2,16640]{2,1,0:T(2,128)(2,1)}), bf16[16,2,16640]{2,1,0:T(2,128)(2,1)}) %all-gather.4.cloned.1.call-update) | async-done | bytes 1064976 | tf_op jit(solution)/shard_map/while/body/eval_jaxpr/all_gather | solution.py:13
  678.2 33.2 %all-gather.4.cloned.1.call-done = bf16[16,2,16640]{2,1,0:T(2,128)(2,1)} async-done(((bf16[1,2,16640]{2,1,0:T(2,128)(2,1)}), bf16[16,2,16640]{2,1,0:T(2,128)(2,1)}) %all-gather.4.cloned.1.call-update) | async-done | bytes 1064976 | tf_op jit(solution)/shard_map/while/body/eval_jaxpr/all_gather | solution.py:13
  717.9 20.3 %all-reduce.8 = (f32[128]{0:T(128)S(1)}, f32[128]{0:T(128)S(1)}) all-reduce(f32[128]{0:T(128)S(1)} %dynamic-update-slice.6, f32[128]{0:T(128)S(1)} %dynamic-update-slice.7), channel_id=2, replica_groups=mesh['dom'=16,'cls'=8] {'cls'}, use_global_device_ids=true, to_apply=%add | all-reduce | flops 256 | bytes 2048 | tf_op jit(solution)/shard_map/while
  740.9 32.9 %all-gather.4.cloned.1.call-done = bf16[16,2,16640]{2,1,0:T(2,128)(2,1)} async-done(((bf16[1,2,16640]{2,1,0:T(2,128)(2,1)}), bf16[16,2,16640]{2,1,0:T(2,128)(2,1)}) %all-gather.4.cloned.1.call-update) | async-done | bytes 1064976 | tf_op jit(solution)/shard_map/while/body/eval_jaxpr/all_gather | solution.py:13
  780.3 20.3 %all-reduce.8 = (f32[128]{0:T(128)S(1)}, f32[128]{0:T(128)S(1)}) all-reduce(f32[128]{0:T(128)S(1)} %dynamic-update-slice.6, f32[128]{0:T(128)S(1)} %dynamic-update-slice.7), channel_id=2, replica_groups=mesh['dom'=16,'cls'=8] {'cls'}, use_global_device_ids=true, to_apply=%add | all-reduce | flops 256 | bytes 2048 | tf_op jit(solution)/shard_map/while
  803.3 33.2 %all-gather.4.cloned.1.call-done = bf16[16,2,16640]{2,1,0:T(2,128)(2,1)} async-done(((bf16[1,2,16640]{2,1,0:T(2,128)(2,1)}), bf16[16,2,16640]{2,1,0:T(2,128)(2,1)}) %all-gather.4.cloned.1.call-update) | async-done | bytes 1064976 | tf_op jit(solution)/shard_map/while/body/eval_jaxpr/all_gather | solution.py:13
  866.1 32.9 %all-gather.4.cloned.1.call-done = bf16[16,2,16640]{2,1,0:T(2,128)(2,1)} async-done(((bf16[1,2,16640]{2,1,0:T(2,128)(2,1)}), bf16[16,2,16640]{2,1,0:T(2,128)(2,1)}) %all-gather.4.cloned.1.call-update) | async-done | bytes 1064976 | tf_op jit(solution)/shard_map/while/body/eval_jaxpr/all_gather | solution.py:13
  928.5 32.9 %all-gather.4.cloned.1.call-done = bf16[16,2,16640]{2,1,0:T(2,128)(2,1)} async-done(((bf16[1,2,16640]{2,1,0:T(2,128)(2,1)}), bf16[16,2,16640]{2,1,0:T(2,128)(2,1)}) %all-gather.4.cloned.1.call-update) | async-done | bytes 1064976 | tf_op jit(solution)/shard_map/while/body/eval_jaxpr/all_gather | solution.py:13
  991.0 32.9 %all-gather.4.cloned.1.call-done = bf16[16,2,16640]{2,1,0:T(2,128)(2,1)} async-done(((bf16[1,2,16640]{2,1,0:T(2,128)(2,1)}), bf16[16,2,16640]{2,1,0:T(2,128)(2,1)}) %all-gather.4.cloned.1.call-update) | async-done | bytes 1064976 | tf_op jit(solution)/shard_map/while/body/eval_jaxpr/all_gather | solution.py:13
  1051.3 126.5 %while.89 = (s32[]{:T(128)}, f32[16,2,16640]{2,1,0:T(2,128)}, f32[16,2]{1,0:T(8,128)S(1)}, f32[16,8320]{1,0:T(8,128)S(1)}, s32[16]{0:T(128)S(1)}, /*index=5*/f32...) while((s32[]{:T(128)}, f32[16,2,16640]{2,1,0:T(2,128)}, ...), condition=%wide.region_12.13_spmd, body=%wide.region_8.12_spmd.sunk | while | flops 138461184 | bytes 10018055 | solution.py:129
  1179.0 31.1 %all-reduce.5 = f32[16,2]{1,0:T(8,128)S(1)} all-reduce(f32[16,2]{1,0:T(8,128)S(1)} %get-tuple-element.557), channel_id=5, replica_groups=mesh['dom'=16,'cls'=8] {'dom'}, use_global_device_ids=true, to_apply=%region_14.15.clone | all-reduce | flops 32 | bytes 256
  1211.3 89.2 %all-reduce.11.cloned.1.call-done = f32[16,2,16640]{2,1,0:T(2,128)} async-done(((f32[16,2,16640]{2,1,0:T(2,128)}), f32[16,2,16640]{2,1,0:T(2,128)}) %all-reduce.11.cloned.1.call-update) | async-done | bytes 2129936
  (608 shorter events, 519.5 us)
Async XLA Ops:
  28.6 17.1 %copy-start = (f32[8320]{0:T(1024)S(1)}, f32[8320]{0:T(1024)}, u32[]{:S(2)}) copy-start(f32[8320]{0:T(1024)} %param.14) | copy-start | bytes 99844
  28.6 17.1 %copy-start.1 = (bf16[1,2,16640]{2,1,0:T(2,128)(2,1)S(1)}, bf16[1,2,16640]{2,1,0:T(2,128)(2,1)}, u32[]{:S(2)}) copy-start(bf16[1,2,16640]{2,1,0:T(2,128)(2,1)} %param.13) | copy-start | bytes 199684
  28.6 17.1 %copy-start.3 = (s32[16]{0:T(128)S(1)}, s32[16]{0:T(128)}, u32[]{:S(2)}) copy-start(s32[16]{0:T(128)} %param.17) | copy-start | bytes 196
  28.6 17.1 %copy-start.4 = (s32[16]{0:T(128)S(1)}, s32[16]{0:T(128)}, u32[]{:S(2)}) copy-start(s32[16]{0:T(128)} %param.16) | copy-start | bytes 196
  28.6 17.1 %copy-start.6 = (u32[128]{0:T(128)S(1)}, u32[128]{0:T(128)}, u32[]{:S(2)}) copy-start(u32[128]{0:T(128)} %constant.327) | copy-start | bytes 1540
  45.7 39.4 %all-gather.4.cloned.1.call-start = ((), (), s32[]{:S(2)}) async-start(), calls=%async_computation.1 | async-start | bytes 1131520 | tf_op jit(solution)/shard_map/while/body/eval_jaxpr/all_gather | solution.py:13
  112.5 35.4 %all-gather.4.cloned.1.call-start = ((), (), s32[]{:S(2)}) async-start(), calls=%async_computation.1 | async-start | bytes 1131520 | tf_op jit(solution)/shard_map/while/body/eval_jaxpr/all_gather | solution.py:13
  175.2 35.4 %all-gather.4.cloned.1.call-start = ((), (), s32[]{:S(2)}) async-start(), calls=%async_computation.1 | async-start | bytes 1131520 | tf_op jit(solution)/shard_map/while/body/eval_jaxpr/all_gather | solution.py:13
  238.0 35.1 %all-gather.4.cloned.1.call-start = ((), (), s32[]{:S(2)}) async-start(), calls=%async_computation.1 | async-start | bytes 1131520 | tf_op jit(solution)/shard_map/while/body/eval_jaxpr/all_gather | solution.py:13
  300.4 35.1 %all-gather.4.cloned.1.call-start = ((), (), s32[]{:S(2)}) async-start(), calls=%async_computation.1 | async-start | bytes 1131520 | tf_op jit(solution)/shard_map/while/body/eval_jaxpr/all_gather | solution.py:13
  362.8 35.1 %all-gather.4.cloned.1.call-start = ((), (), s32[]{:S(2)}) async-start(), calls=%async_computation.1 | async-start | bytes 1131520 | tf_op jit(solution)/shard_map/while/body/eval_jaxpr/all_gather | solution.py:13
  425.3 35.4 %all-gather.4.cloned.1.call-start = ((), (), s32[]{:S(2)}) async-start(), calls=%async_computation.1 | async-start | bytes 1131520 | tf_op jit(solution)/shard_map/while/body/eval_jaxpr/all_gather | solution.py:13
  488.0 35.4 %all-gather.4.cloned.1.call-start = ((), (), s32[]{:S(2)}) async-start(), calls=%async_computation.1 | async-start | bytes 1131520 | tf_op jit(solution)/shard_map/while/body/eval_jaxpr/all_gather | solution.py:13
  550.8 35.4 %all-gather.4.cloned.1.call-start = ((), (), s32[]{:S(2)}) async-start(), calls=%async_computation.1 | async-start | bytes 1131520 | tf_op jit(solution)/shard_map/while/body/eval_jaxpr/all_gather | solution.py:13
  613.5 35.1 %all-gather.4.cloned.1.call-start = ((), (), s32[]{:S(2)}) async-start(), calls=%async_computation.1 | async-start | bytes 1131520 | tf_op jit(solution)/shard_map/while/body/eval_jaxpr/all_gather | solution.py:13
  676.0 35.4 %all-gather.4.cloned.1.call-start = ((), (), s32[]{:S(2)}) async-start(), calls=%async_computation.1 | async-start | bytes 1131520 | tf_op jit(solution)/shard_map/while/body/eval_jaxpr/all_gather | solution.py:13
  738.7 35.1 %all-gather.4.cloned.1.call-start = ((), (), s32[]{:S(2)}) async-start(), calls=%async_computation.1 | async-start | bytes 1131520 | tf_op jit(solution)/shard_map/while/body/eval_jaxpr/all_gather | solution.py:13
  801.1 35.4 %all-gather.4.cloned.1.call-start = ((), (), s32[]{:S(2)}) async-start(), calls=%async_computation.1 | async-start | bytes 1131520 | tf_op jit(solution)/shard_map/while/body/eval_jaxpr/all_gather | solution.py:13
  863.9 35.1 %all-gather.4.cloned.1.call-start = ((), (), s32[]{:S(2)}) async-start(), calls=%async_computation.1 | async-start | bytes 1131520 | tf_op jit(solution)/shard_map/while/body/eval_jaxpr/all_gather | solution.py:13
  926.3 35.1 %all-gather.4.cloned.1.call-start = ((), (), s32[]{:S(2)}) async-start(), calls=%async_computation.1 | async-start | bytes 1131520 | tf_op jit(solution)/shard_map/while/body/eval_jaxpr/all_gather | solution.py:13
  988.8 35.1 %all-gather.4.cloned.1.call-start = ((), (), s32[]{:S(2)}) async-start(), calls=%async_computation.1 | async-start | bytes 1131520 | tf_op jit(solution)/shard_map/while/body/eval_jaxpr/all_gather | solution.py:13
  1051.2 249.3 %all-reduce.11.cloned.1.call-start = ((), (), s32[]{:S(2)}) async-start(), calls=%async_computation | async-start | bytes 4259840
  1177.7 124.9 %copy-start.2 = (f32[16]{0:T(128)}, f32[16]{0:T(128)S(1)}, u32[]{:S(2)}) copy-start(f32[16]{0:T(128)S(1)} %get-tuple-element.1022) | copy-start | bytes 196
  1177.8 0.7 copy-start.5
Sparse Core Ops, SparseCore 0:
  49.0 36.1 all-gather.3
  115.7 32.1 all-gather.3
  178.5 32.1 all-gather.3
  240.9 32.1 all-gather.3
  303.3 32.1 all-gather.3
  365.8 32.1 all-gather.3
  428.5 32.1 all-gather.3
  491.3 32.1 all-gather.3
  554.0 32.1 all-gather.3
  616.5 32.1 all-gather.3
  679.2 32.1 all-gather.3
  741.6 32.1 all-gather.3
  804.4 32.1 all-gather.3
  866.8 32.1 all-gather.3
  929.3 32.1 all-gather.3
  991.7 32.1 all-gather.3
Sparse Core Ops, SparseCore 1:
  1177.9 122.5 all-reduce.10
